TPU v7x, 128 devices: a whole 4x4x4 slice. The times are simulated.
128 devices in a mesh: row: 32 (over x_hi, z, y), ch: 4 (over x_lo, core).
Axes of the slice: x: 4 (x_hi: 2, x_lo: 2; x = x_hi * 2 + x_lo), y: 4, z: 4, core: 2. Of those that a mesh axis runs over, the one named last changes fastest.
Arguments:
- pair_rep: float32 [256, 256, 128], P(('row', 'ch')), may hold values from -6 to 6
- pair_mask: int32 [256, 256], P(('row', 'ch')), may hold values from 0 to 1, as said below
- ln_in_gain: float32 [128], replicated, may hold values from 0.5 to 1.5
- ln_in_bias: float32 [128], replicated, may hold values from -3 to 3
- w_in: float32 [128, 640], replicated, may hold values from -0.5 to 0.5
- b_in: float32 [640], replicated, may hold values from -3 to 3
- ln_out_gain: float32 [128], replicated, may hold values from 0.5 to 1.5
- ln_out_bias: float32 [128], replicated, may hold values from -3 to 3
- w_out: float32 [128, 128], replicated, may hold values from -0.5 to 0.5
- b_out: float32 [128], replicated, may hold values from -3 to 3
- cotangent: float32 [256, 256, 128], P(('row', 'ch')), may hold values from -6 to 6
Outputs:
- update: float32 [256, 256, 128], P(('row', 'ch'))
- grad_pair: float32 [256, 256, 128], P(('row', 'ch'))
- grad_w_in: float32 [128, 640], replicated
- grad_w_out: float32 [128, 128], replicated
Inputs may be any that keep to these rules, and one draw needn't show every extreme that they name: pair_mask[i, k] = m_i m_k, where m is 1 for the residues present in the crop and 0 otherwise.
All inputs are finite; a program needn't handle non-finite values.
Results may differ from a plain program's by a relative error of at most 0.00009.
Values sent between devices are 32-bit elements; how exact they have to be, the bound alone decides.
No kernel may reach another device: no remote copies, remote signals or barrier semaphores. Data moves between devices by JAX's collectives and lax.ppermute only.
A program may use at most 64 MiB of HBM per device.

v0:
```python
import jax
import jax.numpy as jnp
from jax import lax
from jax.sharding import PartitionSpec as P

epsilon = 1e-05


def side_by_side(arrays, axis, split_dim, concat_dim, along):
    ends, at = ([], 0)
    for a in arrays[:-1]:
        at += a.shape[along]
        ends.append(at)
    both = jnp.concatenate(arrays, axis=along)
    return tuple(
        jnp.split(
            lax.all_to_all(both, axis, split_axis=split_dim, concat_axis=concat_dim, tiled=True),
            ends,
            axis=along,
        )
    )


def prelude(field, keep_mask, norm_gain, norm_bias, weights, offsets):
    channels = field.shape[-1]
    hidden = (weights.shape[1] - channels) // 4
    center = jnp.mean(field, -1, keepdims=True)
    spread = jnp.mean((field - center) ** 2, -1, keepdims=True)
    normed = (field - center) * lax.rsqrt(spread + epsilon) * norm_gain + norm_bias
    pieces = jnp.einsum(
        "ikc,cf->fik", normed, weights[:, : 4 * hidden], precision=lax.Precision.HIGHEST
    )
    pieces = pieces + offsets[: 4 * hidden, None, None]
    gate = jax.nn.sigmoid(
        jnp.einsum("ikc,cf->ikf", normed, weights[:, 4 * hidden :], precision=lax.Precision.HIGHEST)
        + offsets[4 * hidden :]
    )
    keep = keep_mask.astype(field.dtype)[None]
    left = keep * jax.nn.sigmoid(pieces[:hidden]) * pieces[hidden : 2 * hidden]
    right = keep * jax.nn.sigmoid(pieces[2 * hidden : 3 * hidden]) * pieces[3 * hidden :]
    return (left, right, gate)


def epilogue(product, gate, norm_gain, norm_bias, weights, offset):
    center = jnp.mean(product, 0, keepdims=True)
    spread = jnp.mean((product - center) ** 2, 0, keepdims=True)
    normed = (product - center) * lax.rsqrt(spread + epsilon) * norm_gain[
        :, None, None
    ] + norm_bias[:, None, None]
    projected = jnp.einsum("hij,hc->ijc", normed, weights, precision=lax.Precision.HIGHEST) + offset
    return gate * projected


def on_device(
    pair_rep,
    pair_mask,
    ln_in_gain,
    ln_in_bias,
    w_in,
    b_in,
    ln_out_gain,
    ln_out_bias,
    w_out,
    b_out,
    cotangent,
):
    row_count = pair_rep.shape[0]
    length = pair_rep.shape[1]
    hidden = w_out.shape[0]
    per_device = hidden // (lax.axis_size("row") * lax.axis_size("ch"))

    def local_prelude(field, weights):
        return prelude(field, pair_mask, ln_in_gain, ln_in_bias, weights, b_in)

    (left_rows, right_rows, gate), prelude_back = jax.vjp(local_prelude, pair_rep, w_in)
    row_shape = (hidden, 1, row_count, length)
    left_cols, right_cols = side_by_side(
        (left_rows.reshape(row_shape), right_rows.reshape(row_shape)), ("row", "ch"), 0, 2, 1
    )
    left_cols = left_cols.reshape(per_device, length, length)
    right_cols = right_cols.reshape(per_device, length, length)
    product = jnp.einsum("hik,hjk->hij", left_cols, right_cols, precision=lax.Precision.HIGHEST)
    product_rows = lax.all_to_all(
        product.reshape(per_device, 1, length, length),
        ("row", "ch"),
        split_axis=2,
        concat_axis=0,
        tiled=True,
    )
    product_rows = product_rows.reshape(hidden, row_count, length)

    def local_epilogue(prod_part, gate_part, weights):
        return epilogue(prod_part, gate_part, ln_out_gain, ln_out_bias, weights, b_out)

    update, epilogue_back = jax.vjp(local_epilogue, product_rows, gate, w_out)
    d_product, d_gate, d_wout = epilogue_back(cotangent)
    d_cols = lax.all_to_all(
        d_product.reshape(row_shape), ("row", "ch"), split_axis=0, concat_axis=2, tiled=True
    )
    d_cols = d_cols.reshape(per_device, length, length)
    d_left = jnp.einsum("hij,hjk->hik", d_cols, right_cols, precision=lax.Precision.HIGHEST)
    d_right = jnp.einsum("hij,hik->hjk", d_cols, left_cols, precision=lax.Precision.HIGHEST)
    col_shape = (per_device, 1, length, length)
    d_left, d_right = side_by_side(
        (d_left.reshape(col_shape), d_right.reshape(col_shape)), ("row", "ch"), 2, 0, 1
    )
    d_left = d_left.reshape(hidden, row_count, length)
    d_right = d_right.reshape(hidden, row_count, length)
    grad_pair, d_win = prelude_back((d_left, d_right, d_gate))
    d_win, d_wout = lax.psum((d_win, d_wout), ("row", "ch"))
    return (update, grad_pair, d_win / length, d_wout / length)


def solution(mesh):
    placed = (
        P(("row", "ch"), None, None),
        P(("row", "ch"), None),
        P(),
        P(),
        P(),
        P(),
        P(),
        P(),
        P(),
        P(),
        P(("row", "ch"), None, None),
    )
    return jax.shard_map(
        on_device,
        mesh=mesh,
        in_specs=placed,
        out_specs=(P(("row", "ch"), None, None), P(("row", "ch"), None, None), P(), P()),
        check_vma=False,
    )
```

profile of v0, /device:TPU:1, one launch (start us, length us, event | category | flops | bytes accessed | tf_op | source)
XLA Modules:
  0.0 247.7 jit_solution(5997997700631045639)
XLA Ops:
  7.2 0.7 convert_element_type.3
  7.9 1.1 copy.48
  9.3 0.7 copy-done.3
  10.0 1.1 fusion
  11.6 24.7 %all_to_all.54 = f32[128,2,2,256]{3,2,1,0:T(2,128)S(1)} all-to-all(f32[128,2,2,256]{3,2,1,0:T(2,128)S(1)} %copy.51), channel_id=1, replica_groups=mesh['row'=32,'ch'=4] {'row','ch'}, dimensions={0} | all-to-all | bytes 1048576 | tf_op jit(solution)/shard_map/all_to_all | solution.py:17
  36.7 0.4 fusion.51
  37.1 0.4 convolution_bitcast_fusion.2
  37.5 1.0 copy.53
  38.5 4.9 %all-to-all-start.1 = ((f32[1,1,256,256]{3,1,0,2:T(1,128)}), f32[1,1,256,256]{3,1,0,2:T(1,128)S(1)}, u32[]{:S(2)}, u32[]{:S(2)}) async-start(f32[1,1,256,256]{3,1,0,2:T(1,128)} %copy.53), calls=%async_computation.1 | async-start | bytes 524288 | tf_op jit(solution)/shard_map/all_to_all | solution.py:83
  43.4 0.7 fusion.6
  44.1 10.3 %all-to-all-done.1 = f32[1,1,256,256]{3,1,0,2:T(1,128)S(1)} async-done(((f32[1,1,256,256]{3,1,0,2:T(1,128)}), f32[1,1,256,256]{3,1,0,2:T(1,128)S(1)}, u32[]{:S(2)}, u32[]{:S(2)}) %all-to-all-start.1) | async-done | bytes 262176 | tf_op jit(solution)/shard_map/all_to_all | solution.py:83
  54.3 0.6 reduce
  55.3 0.8 copy-done.1
  56.1 0.4 multiply_reduce_fusion.1
  56.9 15.3 %all_to_all.55 = f32[128,1,2,256]{3,2,1,0:T(2,128)S(1)} all-to-all(f32[128,1,2,256]{3,2,1,0:T(2,128)S(1)} %copy.56), channel_id=1, replica_groups=mesh['row'=32,'ch'=4] {'row','ch'}, dimensions={0} | all-to-all | bytes 524288 | tf_op jit(solution)/shard_map/all_to_all | solution.py:97
  72.4 0.6 convolution_bitcast_fusion
  73.0 0.4 convolution_bitcast_fusion.1
  73.4 1.2 copy.57
  74.6 4.5 %all-to-all-start.3 = ((f32[1,2,256,256]{3,1,0,2:T(2,128)}), f32[1,2,256,256]{3,1,0,2:T(2,128)S(1)}, u32[]{:S(2)}, u32[]{:S(2)}) async-start(f32[1,2,256,256]{3,1,0,2:T(2,128)} %copy.57), calls=%async_computation.3 | async-start | bytes 1048576 | tf_op jit(solution)/shard_map/all_to_all | solution.py:17
  79.4 1.1 convolution_bitcast_fusion.4
  80.4 1.4 fusion.52
  81.8 0.5 convolution_bitcast_fusion.5
  82.3 10.3 %all-to-all-done.3 = f32[1,2,256,256]{3,1,0,2:T(2,128)S(1)} async-done(((f32[1,2,256,256]{3,1,0,2:T(2,128)}), f32[1,2,256,256]{3,1,0,2:T(2,128)S(1)}, u32[]{:S(2)}, u32[]{:S(2)}) %all-to-all-start.3) | async-done | bytes 524320 | tf_op jit(solution)/shard_map/all_to_all | solution.py:17
  93.1 0.6 copy-done.8
  93.7 0.8 convolution_bitcast_fusion.3
  94.7 1.2 fusion.7
  95.9 0.5 multiply_reduce_fusion.5
  96.5 0.7 pad_add_fusion.3
  97.3 0.8 copy.61
  98.2 140.3 %all-reduce.9.cloned.1.call-done = (f32[128,640]{1,0:T(8,128)}, f32[128,128]{1,0:T(8,128)}) async-done(((f32[128,640]{1,0:T(8,128)}, f32[128,128]{1,0:T(8,128)}), (f32[128,640]{1,0:T(8,128)}, f32[128,128]{1,0:T(8,128)})) %all-reduce.9.cloned.1.call-update) | async-done | bytes 393232 | tf_op jit(solution)/shard_map/psum | solution.py:110
  238.4 1.8 broadcast_multiply_fusion
  240.2 0.6 broadcast_multiply_fusion.1
  (54 shorter events, 2.9 us)
Async XLA Ops:
  7.2 48.1 %copy-start = (f32[128,128]{1,0:T(8,128)S(1)}, f32[128,128]{1,0:T(8,128)}, u32[]{:S(2)}) copy-start(f32[128,128]{1,0:T(8,128)} %param.19) | copy-start | bytes 196612
  7.9 1.2 copy-start.2
  9.1 1.0 copy-start.3
  9.3 0.8 slice-start
  9.3 0.7 copy-start.7
  9.3 0.7 copy-start.10
  38.5 4.9 %copy-start.6 = (f32[640]{0:T(1024)S(1)}, f32[640]{0:T(1024)}, u32[]{:S(2)}) copy-start(f32[640]{0:T(1024)} %param.16) | copy-start | bytes 7684
  38.5 15.9 %all-to-all-start.1 = ((f32[1,1,256,256]{3,1,0,2:T(1,128)}), f32[1,1,256,256]{3,1,0,2:T(1,128)S(1)}, u32[]{:S(2)}, u32[]{:S(2)}) async-start(f32[1,1,256,256]{3,1,0,2:T(1,128)} %copy.53), calls=%async_computation.1 | async-start | bytes 524288 | tf_op jit(solution)/shard_map/all_to_all | solution.py:83
  55.1 1.0 copy-start.1
  55.3 0.8 copy-start.9
  74.6 4.8 %copy-start.12 = (f32[128]{0:T(128)S(1)}, f32[128]{0:T(128)}, u32[]{:S(2)}) copy-start(f32[128]{0:T(128)} %param.18) | copy-start | bytes 1540
  74.6 18.0 %all-to-all-start.3 = ((f32[1,2,256,256]{3,1,0,2:T(2,128)}), f32[1,2,256,256]{3,1,0,2:T(2,128)S(1)}, u32[]{:S(2)}, u32[]{:S(2)}) async-start(f32[1,2,256,256]{3,1,0,2:T(2,128)} %copy.57), calls=%async_computation.3 | async-start | bytes 1048576 | tf_op jit(solution)/shard_map/all_to_all | solution.py:17
  79.1 1.3 copy-start.13
  79.1 159.3 %all-reduce.9.cloned.1.call-start = ((), (), s32[]{:S(2)}) async-start(), calls=%async_computation.4 | async-start | bytes 786432 | tf_op jit(solution)/shard_map/psum | solution.py:110
  93.1 0.7 copy-start.8
  93.1 0.7 copy-start.11
  93.7 1.0 copy-start.4
  238.4 1.8 copy-start.5
Sparse Core Ops, SparseCore 0:
  97.4 141.0 all-reduce.8
where the time goes:
time: 248 us
  waiting for transfers between devices  161 us (65%)
  blocking collectives  40 us (16%)
  between operations  14.4 us (6%)
  starting transfers between devices  9.62 us (4%)
  matrix products  8.93 us (4%)
  local copies, waits for them, and re-layouts  8.28 us (3%)
  other arithmetic  5.56 us (2%)
    psum x1, waiting for transfers between devices, on_device(): d_win, d_wout = lax.psum((d_win, d_wout), ('row', 'ch'))  140 us
    all_to_all x1, blocking collectives, side_by_side(): lax.all_to_all(both, axis, split_axis=split_dim, concat_axis=concat_dim,...  24.7 us
    all_to_all x1, blocking collectives, on_device(): lax.all_to_all(d_product.reshape(row_shape), ('row', 'ch'), split_axis=0,...  15.3 us
    all_to_all x1, waiting for transfers between devices, side_by_side(): lax.all_to_all(both, axis, split_axis=split_dim, concat_axis=concat_dim,...  10.3 us
    all_to_all x1, waiting for transfers between devices, on_device(): lax.all_to_all(product.reshape(per_device, 1, length, length), ('row', 'c...  10.3 us
  transfers between devices with their start and end apart: 3, of which 3 were waited for; matrix products, arithmetic and copies ran while one was open for 2% of the time, Pallas kernels for 0%

commit v1 on v0

--- a/solution.py
+++ b/solution.py
@@ -4,6 +4,11 @@
 from jax.sharding import PartitionSpec as P
 
 epsilon = 1e-05
+
+
+def by_each_axis(array, one, other):
+    half = lax.psum(array, one)
+    return lax.psum(half, other)
 
 
 def side_by_side(arrays, axis, split_dim, concat_dim, along):
@@ -107,7 +112,7 @@
     d_left = d_left.reshape(hidden, row_count, length)
     d_right = d_right.reshape(hidden, row_count, length)
     grad_pair, d_win = prelude_back((d_left, d_right, d_gate))
-    d_win, d_wout = lax.psum((d_win, d_wout), ("row", "ch"))
+    d_win, d_wout = by_each_axis((d_win, d_wout), "row", "ch")
     return (update, grad_pair, d_win / length, d_wout / length)
 
 

time: 248 us -> 480 us (1.94)
  waiting for transfers between devices: 161 us -> 393 us
    psum x1 -> x2, waiting for transfers between devices: 140 us -> 372 us  [the longest x1 315 us: by_each_axis(): half = lax.psum(array, one)]
  transfers between devices with their start and end apart: 3 -> 4, of which waited for: 3 -> 4; matrix products, arithmetic and copies ran while one was open for 2% -> 1% of each run, Pallas kernels for 0% -> 0%
where the time goes in v1:
time: 480 us
  waiting for transfers between devices  393 us (82%)
  blocking collectives  40 us (8%)
  between operations  14.4 us (3%)
  starting transfers between devices  9.67 us (2%)
  matrix products  8.92 us (2%)
  local copies, waits for them, and re-layouts  8.28 us (2%)
  other arithmetic  5.56 us (1%)
    psum x1, waiting for transfers between devices, by_each_axis(): half = lax.psum(array, one)  315 us
    psum x1, waiting for transfers between devices, by_each_axis(): return lax.psum(half, other)  56.9 us
    all_to_all x1, blocking collectives, side_by_side(): lax.all_to_all(both, axis, split_axis=split_dim, concat_axis=concat_dim,...  24.7 us
    all_to_all x1, blocking collectives, on_device(): lax.all_to_all(d_product.reshape(row_shape), ('row', 'ch'), split_axis=0,...  15.3 us
    all_to_all x1, waiting for transfers between devices, side_by_side(): lax.all_to_all(both, axis, split_axis=split_dim, concat_axis=concat_dim,...  10.3 us
    all_to_all x1, waiting for transfers between devices, on_device(): lax.all_to_all(product.reshape(per_device, 1, length, length), ('row', 'c...  10.3 us
  transfers between devices with their start and end apart: 4, of which 4 were waited for; matrix products, arithmetic and copies ran while one was open for 1% of the time, Pallas kernels for 0%

profile of v1, /device:TPU:1, one launch (start us, length us, event | category | flops | bytes accessed | tf_op | source)
XLA Modules:
  0.0 479.7 jit_solution(8070673602340824726)
XLA Ops:
  7.2 0.7 convert_element_type.3
  7.9 1.1 copy.48
  9.3 0.7 copy-done.3
  10.0 1.1 fusion
  11.6 24.7 %all_to_all.54 = f32[128,2,2,256]{3,2,1,0:T(2,128)S(1)} all-to-all(f32[128,2,2,256]{3,2,1,0:T(2,128)S(1)} %copy.51), channel_id=1, replica_groups=mesh['row'=32,'ch'=4] {'row','ch'}, dimensions={0} | all-to-all | bytes 1048576 | tf_op jit(solution)/shard_map/all_to_all | solution.py:22
  36.7 0.4 fusion.51
  37.1 0.4 convolution_bitcast_fusion.2
  37.5 1.0 copy.53
  38.5 4.9 %all-to-all-start.1 = ((f32[1,1,256,256]{3,1,0,2:T(1,128)}), f32[1,1,256,256]{3,1,0,2:T(1,128)S(1)}, u32[]{:S(2)}, u32[]{:S(2)}) async-start(f32[1,1,256,256]{3,1,0,2:T(1,128)} %copy.53), calls=%async_computation.1 | async-start | bytes 524288 | tf_op jit(solution)/shard_map/all_to_all | solution.py:88
  43.4 0.7 fusion.6
  44.1 10.3 %all-to-all-done.1 = f32[1,1,256,256]{3,1,0,2:T(1,128)S(1)} async-done(((f32[1,1,256,256]{3,1,0,2:T(1,128)}), f32[1,1,256,256]{3,1,0,2:T(1,128)S(1)}, u32[]{:S(2)}, u32[]{:S(2)}) %all-to-all-start.1) | async-done | bytes 262176 | tf_op jit(solution)/shard_map/all_to_all | solution.py:88
  54.3 0.6 reduce
  55.3 0.8 copy-done.1
  56.1 0.4 multiply_reduce_fusion.1
  56.9 15.3 %all_to_all.55 = f32[128,1,2,256]{3,2,1,0:T(2,128)S(1)} all-to-all(f32[128,1,2,256]{3,2,1,0:T(2,128)S(1)} %copy.56), channel_id=1, replica_groups=mesh['row'=32,'ch'=4] {'row','ch'}, dimensions={0} | all-to-all | bytes 524288 | tf_op jit(solution)/shard_map/all_to_all | solution.py:102
  72.4 0.6 convolution_bitcast_fusion
  73.4 1.2 copy.57
  74.6 4.5 all-to-all-start.3
  79.4 1.1 convolution_bitcast_fusion.4
  80.4 1.4 fusion.52
  81.8 0.5 convolution_bitcast_fusion.5
  82.3 10.3 %all-to-all-done.3 = f32[1,2,256,256]{3,1,0,2:T(2,128)S(1)} async-done(((f32[1,2,256,256]{3,1,0,2:T(2,128)}), f32[1,2,256,256]{3,1,0,2:T(2,128)S(1)}, u32[]{:S(2)}, u32[]{:S(2)}) %all-to-all-start.3) | async-done | bytes 524320 | tf_op jit(solution)/shard_map/all_to_all | solution.py:22
  93.1 0.6 copy-done.8
  93.7 0.8 convolution_bitcast_fusion.3
  94.7 1.2 fusion.7
  95.9 0.7 pad_add_fusion.3
  96.7 0.5 multiply_reduce_fusion.5
  97.3 315.4 %all-reduce.11.cloned.1.call-done = (f32[128,640]{1,0:T(8,128)}, f32[128,128]{1,0:T(8,128)}) async-done(((f32[128,640]{1,0:T(8,128)}, f32[128,128]{1,0:T(8,128)}), (f32[128,640]{1,0:T(8,128)}, f32[128,128]{1,0:T(8,128)})) %all-reduce.11.cloned.1.call-update) | async-done | bytes 393232 | tf_op jit(solution)/shard_map/psum | solution.py:10
  412.8 0.8 copy.61
  413.6 56.9 %all-reduce.13.cloned.1.call-done = (f32[128,640]{1,0:T(8,128)}, f32[128,128]{1,0:T(8,128)}) async-done(((f32[128,640]{1,0:T(8,128)}, f32[128,128]{1,0:T(8,128)}), (f32[128,640]{1,0:T(8,128)}, f32[128,128]{1,0:T(8,128)})) %all-reduce.13.cloned.1.call-update) | async-done | bytes 393232 | tf_op jit(solution)/shard_map/psum | solution.py:11
  470.5 1.8 broadcast_multiply_fusion
  472.3 0.6 broadcast_multiply_fusion.1
  (57 shorter events, 3.4 us)
Async XLA Ops:
  7.2 48.1 %copy-start = (f32[128,128]{1,0:T(8,128)S(1)}, f32[128,128]{1,0:T(8,128)}, u32[]{:S(2)}) copy-start(f32[128,128]{1,0:T(8,128)} %param.19) | copy-start | bytes 196612
  7.9 1.2 copy-start.2
  9.1 1.0 copy-start.3
  9.3 0.8 slice-start
  9.3 0.7 copy-start.7
  9.3 0.7 copy-start.10
  38.5 4.9 %copy-start.6 = (f32[640]{0:T(1024)S(1)}, f32[640]{0:T(1024)}, u32[]{:S(2)}) copy-start(f32[640]{0:T(1024)} %param.16) | copy-start | bytes 7684
  38.5 15.9 %all-to-all-start.1 = ((f32[1,1,256,256]{3,1,0,2:T(1,128)}), f32[1,1,256,256]{3,1,0,2:T(1,128)S(1)}, u32[]{:S(2)}, u32[]{:S(2)}) async-start(f32[1,1,256,256]{3,1,0,2:T(1,128)} %copy.53), calls=%async_computation.1 | async-start | bytes 524288 | tf_op jit(solution)/shard_map/all_to_all | solution.py:88
  55.1 1.0 copy-start.1
  55.3 0.8 copy-start.9
  74.6 4.8 copy-start.12
  74.6 18.0 %all-to-all-start.3 = ((f32[1,2,256,256]{3,1,0,2:T(2,128)}), f32[1,2,256,256]{3,1,0,2:T(2,128)S(1)}, u32[]{:S(2)}, u32[]{:S(2)}) async-start(f32[1,2,256,256]{3,1,0,2:T(2,128)} %copy.57), calls=%async_computation.3 | async-start | bytes 1048576 | tf_op jit(solution)/shard_map/all_to_all | solution.py:22
  79.1 1.3 copy-start.13
  79.1 333.6 %all-reduce.11.cloned.1.call-start = ((), (), s32[]{:S(2)}) async-start(), calls=%async_computation.4 | async-start | bytes 786432 | tf_op jit(solution)/shard_map/psum | solution.py:10
  93.1 0.7 copy-start.8
  93.1 0.7 copy-start.11
  93.7 1.0 copy-start.4
  96.7 373.8 %all-reduce.13.cloned.1.call-start = ((), (), s32[]{:S(2)}) async-start(), calls=%async_computation.5 | async-start | bytes 786432 | tf_op jit(solution)/shard_map/psum | solution.py:11
  470.5 1.8 copy-start.5
Sparse Core Ops, SparseCore 0:
  96.8 315.8 all-reduce.10
  415.4 55.0 all-reduce.12
